TPU v7x, 128 devices: a whole 4x4x4 slice. The times are simulated.
128 devices in a mesh: row: 16 (over x_hi, y, core), col: 8 (over z, x_lo).
Axes of the slice: x: 4 (x_hi: 2, x_lo: 2; x = x_hi * 2 + x_lo), y: 4, z: 4, core: 2. Of those that a mesh axis runs over, the one named last changes fastest.
Arguments:
- values: float32 [8192, 8192], P('row', 'col'), may hold values from 0 to 10, as said below
- pattern: int32 [64, 64], replicated, may hold values from 0 to 1, as said below
- pruning: int32 [64, 64], replicated, may hold values from 0 to 1, as said below
- owners: int32 [64], replicated, may hold values from 0 to 63, as said below
Outputs:
- expanded: float32 [8192, 8192], P('row', 'col')
Inputs may be any that keep to these rules, and one draw needn't show every extreme that they name: `values`: positive scores. `pattern`: every diagonal block is present. `pruning`: every diagonal block is kept. `owners`: A permutation of the 64 column blocks. Of the 8 column blocks of one index of col, at most 2 are stored at the column blocks of any one index of col, and exactly 2 at those of some index.
All inputs are finite; a program needn't handle non-finite values.
Results may differ from a plain program's by a relative error of at most 0.00065.
Values may be sent and summed in bfloat16 or wider, within the bound.
No kernel may reach another device: no remote copies, remote signals or barrier semaphores. Data moves between devices by JAX's collectives and lax.ppermute only.
A program may use at most 128 MiB of HBM per device.

v0:
```python
import jax
import jax.numpy as jnp
from jax import lax
from jax.sharding import PartitionSpec as P

BLK = 128


def expand_mask(tile, mask, blk):
    rows_in, cols_in = tile.shape
    shaped = tile.reshape(rows_in // blk, blk, cols_in // blk, blk)
    return (shaped * mask.astype(tile.dtype)[:, None, :, None]).reshape(rows_in, cols_in)


def ranks_of(destination):
    width = destination.shape[-1]
    earlier = jnp.arange(width)[:, None] < jnp.arange(width)[None, :]
    same_dest = destination[..., :, None] == destination[..., None, :]
    return jnp.sum(jnp.where(same_dest & earlier, 1, 0), axis=-2).astype(jnp.int32)


def pack_blocks(tile, owners, me_col, ncols, capacity, blk):
    rows_in, cols_in = tile.shape
    width = cols_in // blk
    my_owners = lax.dynamic_slice(owners, (me_col * width,), (width,))
    destination = my_owners // width
    rank = ranks_of(destination)
    slot_ids = jnp.arange(ncols * capacity)
    selector = (
        (destination[None, :] == (slot_ids // capacity)[:, None])
        & (rank[None, :] == (slot_ids % capacity)[:, None])
    ).astype(tile.dtype)
    column_blocks = tile.reshape(rows_in, width, blk)
    outgoing = jnp.einsum(
        "pk,rkb->prb",
        selector,
        column_blocks,
        preferred_element_type=jnp.float32,
        precision=lax.Precision.HIGHEST,
    )
    return outgoing


def unpack_blocks(arrived, owners, me_col, ncols, capacity):
    slot_count, rows_in, blk = arrived.shape
    width = owners.shape[0] // ncols
    table = owners.reshape(ncols, width)
    rank = ranks_of(table // width)
    wanted = me_col * width + jnp.arange(width)
    matches = table[None, :, :] == wanted[:, None, None]
    which_slot = rank[:, :, None] == jnp.arange(capacity)[None, None, :]
    selector = jnp.sum(jnp.where(matches[:, :, :, None] & which_slot[None], 1, 0), axis=2)
    selector = selector.reshape(width, ncols * capacity).astype(arrived.dtype)
    placed = jnp.einsum(
        "sp,prb->rsb",
        selector,
        arrived,
        preferred_element_type=jnp.float32,
        precision=lax.Precision.HIGHEST,
    )
    return placed.reshape(rows_in, width * blk)


def body(values, pattern, pruning, owners):
    rows_dev, cols_dev = values.shape
    blk = BLK
    row_blocks = rows_dev // blk
    col_blocks = cols_dev // blk
    ncols = lax.axis_size("col")
    capacity = max(2, (col_blocks + ncols - 1) // ncols)
    me_row = lax.axis_index("row")
    me_col = lax.axis_index("col")
    local_pattern = lax.dynamic_slice(
        pattern, (me_row * row_blocks, me_col * col_blocks), (row_blocks, col_blocks)
    )
    masked = expand_mask(values, local_pattern, blk)
    colsum_in = lax.psum(jnp.sum(masked, axis=0), "row")
    stochastic = (masked / colsum_in[None, :]).astype(jnp.bfloat16)
    row_panel = lax.all_gather(stochastic, "col", axis=1, tiled=True)
    nodes = row_panel.shape[1]
    pruning_rows = lax.dynamic_slice(
        pruning, (me_row * row_blocks, 0), (row_blocks, pruning.shape[1])
    )
    kept_mask = lax.dynamic_slice_in_dim(pruning_rows, me_col * col_blocks, col_blocks, 1)
    square = jnp.dot(
        row_panel,
        lax.all_gather(stochastic, "row", axis=0, tiled=True),
        preferred_element_type=jnp.float32,
    )
    inflated = expand_mask(square * square, kept_mask, blk)
    colsum_out = lax.psum(jnp.sum(inflated, axis=0), "row")
    normalized = jnp.float32(nodes) * inflated / colsum_out[None, :]
    arrived_out = lax.all_to_all(
        pack_blocks(normalized, owners, me_col, ncols, capacity, blk),
        "col",
        split_axis=0,
        concat_axis=0,
        tiled=True,
    )
    result = unpack_blocks(arrived_out, owners, me_col, ncols, capacity)
    return result


def solution(mesh):
    return jax.shard_map(
        body,
        mesh=mesh,
        in_specs=(P("row", "col"), P(), P(), P()),
        out_specs=P("row", "col"),
        check_vma=False,
    )
```

profile of v0, /device:TPU:0, one launch (start us, length us, event | category | flops | bytes accessed | tf_op | source)
XLA Modules:
  0.0 452.6 jit_solution(7957865634004855820)
XLA Ops:
  6.5 0.0 all-gather.3.cloned.1.call-start
  6.5 0.0 copy-start
  6.5 0.9 dynamic-slice_convert_fusion.1
  7.4 0.2 mul.43
  7.7 0.5 copy-done
  8.1 0.7 fusion.2
  8.8 38.2 %psum.14 = f32[1024]{0:T(1024)S(1)} all-reduce(f32[1024]{0:T(1024)S(1)} %fusion.2), channel_id=1, replica_groups=mesh['row'=16,'col'=8] {'row'}, use_global_device_ids=true, to_apply=%region_2.0 | all-reduce | flops 1024 | bytes 8192 | tf_op jit(solution)/shard_map/psum | solution.py:77
  47.0 3.2 divide_convert_fusion
  50.2 0.0 copy-start.1
  50.2 0.0 all-gather.3.cloned.1.call-update
  50.3 0.0 all-gather.5.cloned.1.call-start
  50.3 0.7 all-gather.5.cloned.1.call-update
  51.0 0.0 copy-done.1
  51.0 0.1 and_select_fusion.2
  51.1 0.8 dynamic-slice_convert_fusion
  51.9 0.1 select_reduce_fusion.2
  52.0 164.6 %all-gather.3.cloned.1.call-done = bf16[512,8192]{1,0:T(8,128)(2,1)} async-done(((bf16[512,1024]{1,0:T(8,128)(2,1)}), bf16[512,8192]{1,0:T(8,128)(2,1)}) %all-gather.3.cloned.1.call-update) | async-done | bytes 8388624 | tf_op jit(solution)/shard_map/all_gather | solution.py:79
  216.6 112.1 %all-gather.5.cloned.1.call-done = bf16[8192,1024]{1,0:T(8,128)(2,1)} async-done(((bf16[512,1024]{1,0:T(8,128)(2,1)}), bf16[8192,1024]{1,0:T(8,128)(2,1)}) %all-gather.5.cloned.1.call-update) | async-done | bytes 16777232 | tf_op jit(solution)/shard_map/all_gather | solution.py:87
  328.7 0.2 mul.47
  328.9 14.8 %fusion.14 = (f32[1024]{0:T(1024)S(1)}, f32[512,1024]{1,0:T(8,128)S(1)}) fusion(f32[64,8,8,128]{3,2,1,0:T(8,128)S(1)} %bitcast.34, bf16[512,8192]{1,0:T(8,128)(2,1)} %all-gather.3.cloned.1.call-done, bf16[8192,1024]{1,0:T(8,128)(2,1)} %all-gather.5.cloned.1.call-done), kind=kOutput, calls=%fused_computation.43 | convolution fusion | flops 8591506432 | bytes 29364224 | tf_op jit(solution)/shard_map/dot_general | solution.py:85
  343.7 33.8 %psum.15 = f32[1024]{0:T(1024)S(1)} all-reduce(f32[1024]{0:T(1024)S(1)} %get-tuple-element.5), channel_id=1, replica_groups=mesh['row'=16,'col'=8] {'row'}, use_global_device_ids=true, to_apply=%region_4.5 | all-reduce | flops 1024 | bytes 8192 | tf_op jit(solution)/shard_map/psum | solution.py:91
  377.6 0.3 divide_bitcast_fusion
  377.8 0.5 copy.21
  378.3 1.9 fusion.5
  380.2 3.3 copy.12
  383.5 5.3 %all-to-all-start = ((f32[16,512,128]{2,1,0:T(8,128)}), f32[16,512,128]{2,1,0:T(8,128)}, u32[]{:S(2)}, u32[]{:S(2)}) async-start(f32[16,512,128]{2,1,0:T(8,128)} %copy.12), calls=%async_computation | async-start | bytes 8388608 | tf_op jit(solution)/shard_map/all_to_all | solution.py:93
  388.8 0.1 eq.99
  388.9 0.1 select_reduce_fusion.1
  389.0 0.1 broadcast_compare_fusion
  389.1 0.4 select_reduce_fusion
  389.5 0.1 copy.14
  389.6 47.6 %all-to-all-done = f32[16,512,128]{2,1,0:T(8,128)} async-done(((f32[16,512,128]{2,1,0:T(8,128)}), f32[16,512,128]{2,1,0:T(8,128)}, u32[]{:S(2)}, u32[]{:S(2)}) %all-to-all-start) | async-done | bytes 4194336 | tf_op jit(solution)/shard_map/all_to_all | solution.py:93
  437.1 6.8 %fusion = f32[512,128,8]{1,2,0:T(8,128)S(1)} fusion(f32[8,16,1]{0,1,2:T(8,128)S(1)} %bitcast.35, f32[16,512,128]{2,1,0:T(8,128)} %all-to-all-done), kind=kOutput, calls=%fused_computation | convolution fusion | flops 100663296 | bytes 6291968 | tf_op jit(solution)/shard_map/sp,prb->rsb/dot_general | solution.py:54
  444.0 1.8 copy.33
  (6 shorter events, 0.0 us)
Async XLA Ops:
  6.5 210.1 %all-gather.3.cloned.1.call-start = ((), (), s32[]{:S(2)}) async-start(), calls=%async_computation.1 | async-start | bytes 9437184 | tf_op jit(solution)/shard_map/all_gather | solution.py:79
  6.5 1.6 copy-start
  50.2 0.8 copy-start.1
  50.3 278.4 %all-gather.5.cloned.1.call-start = ((), (), s32[]{:S(2)}) async-start(), calls=%async_computation.2 | async-start | bytes 17825792 | tf_op jit(solution)/shard_map/all_gather | solution.py:87
  383.5 53.7 %all-to-all-start = ((f32[16,512,128]{2,1,0:T(8,128)}), f32[16,512,128]{2,1,0:T(8,128)}, u32[]{:S(2)}, u32[]{:S(2)}) async-start(f32[16,512,128]{2,1,0:T(8,128)} %copy.12), calls=%async_computation | async-start | bytes 8388608 | tf_op jit(solution)/shard_map/all_to_all | solution.py:93
Sparse Core Ops, SparseCore 0:
  50.4 166.1 all-gather.2
  219.0 109.6 all-gather.4
where the time goes:
time: 453 us
  waiting for transfers between devices  325 us (72%)
  blocking collectives  72 us (16%)
  matrix products  23.5 us (5%)
  between operations  13.5 us (3%)
  other arithmetic  6.6 us (1%)
  local copies, waits for them, and re-layouts  6.55 us (1%)
  starting transfers between devices  5.38 us (1%)
    all_gather x1, waiting for transfers between devices, body(): row_panel = lax.all_gather(stochastic, 'col', axis=1, tiled=True)  165 us
    all_gather x1, waiting for transfers between devices, body(): lax.all_gather(stochastic, 'row', axis=0, tiled=True)  112 us
    all_to_all x1, waiting for transfers between devices, body(): lax.all_to_all(pack_blocks(normalized, owners, me_col, ncols, capacity, b...  47.6 us
    psum x1, blocking collectives, body(): colsum_in = lax.psum(jnp.sum(masked, axis=0), 'row')  38.2 us
    psum x1, blocking collectives, body(): colsum_out = lax.psum(jnp.sum(inflated, axis=0), 'row')  33.8 us
    dot_general x1, matrix products, body(): jnp.dot(row_panel, lax.all_gather(stochastic, 'row', axis=0, tiled=True),...  14.8 us
  transfers between devices with their start and end apart: 3, of which 3 were waited for; matrix products, arithmetic and copies ran while one was open for 0% of the time, Pallas kernels for 0%

commit v1 on v0

--- a/solution.py
+++ b/solution.py
@@ -84,7 +84,9 @@
     kept_mask = lax.dynamic_slice_in_dim(pruning_rows, me_col * col_blocks, col_blocks, 1)
     square = jnp.dot(
         row_panel,
-        lax.all_gather(stochastic, "row", axis=0, tiled=True),
+        jnp.concatenate(
+            lax.all_to_all(jnp.stack([stochastic] * lax.axis_size("row")), "row", 0, 0), axis=0
+        ),
         preferred_element_type=jnp.float32,
     )
     inflated = expand_mask(square * square, kept_mask, blk)

time: 453 us -> 536 us (1.18)
  waiting for transfers between devices: 325 us -> 389 us
  blocking collectives: 72 us -> 78.9 us
  starting transfers between devices: 5.38 us -> 11.7 us
  local copies, waits for them, and re-layouts: 6.55 us -> 12.7 us
    all_gather x1, waiting for transfers between devices: 165 us -> 329 us  [body(): row_panel = lax.all_gather(stochastic, 'col', axis=1, tiled=True)]
    all_gather x1 -> x0, waiting for transfers between devices: 112 us -> none  [body(): lax.all_gather(stochastic, 'row', axis=0, tiled=True)]
    all_to_all x0 -> x1, waiting for transfers between devices: none -> 15.8 us  [body(): lax.all_to_all(jnp.stack([stochastic] * lax.axis_size('row')), 'row', 0, 0)]
    psum x1, blocking collectives: 33.8 us -> 40.7 us  [body(): colsum_out = lax.psum(jnp.sum(inflated, axis=0), 'row')]
    another operation x0 -> x1, local copies, waits for them, and re-layouts: none -> 6.17 us  [body(): jnp.stack([stochastic] * lax.axis_size('row'))]
where the time goes in v1:
time: 536 us; the launch traced here: 535 us
  waiting for transfers between devices  389 us (73%)
  blocking collectives  78.9 us (15%)
  matrix products  23.5 us (4%)
  between operations  13.5 us (3%)
  local copies, waits for them, and re-layouts  12.7 us (2%)
  starting transfers between devices  11.7 us (2%)
  other arithmetic  5.63 us (1%)
    all_gather x1, waiting for transfers between devices, body(): row_panel = lax.all_gather(stochastic, 'col', axis=1, tiled=True)  329 us
    all_to_all x1, waiting for transfers between devices, body(): lax.all_to_all(pack_blocks(normalized, owners, me_col, ncols, capacity, b...  43.8 us
    psum x1, blocking collectives, body(): colsum_out = lax.psum(jnp.sum(inflated, axis=0), 'row')  40.7 us
    psum x1, blocking collectives, body(): colsum_in = lax.psum(jnp.sum(masked, axis=0), 'row')  38.2 us
    all_to_all x1, waiting for transfers between devices, body(): lax.all_to_all(jnp.stack([stochastic] * lax.axis_size('row')), 'row', 0, 0)  15.8 us
    dot_general x1, matrix products, body(): jnp.dot(row_panel, jnp.concatenate(lax.all_to_all(jnp.stack([stochastic]...  14.8 us
  transfers between devices with their start and end apart: 3, of which 3 were waited for; matrix products, arithmetic and copies ran while one was open for 0% of the time, Pallas kernels for 0%

profile of v1, /device:TPU:0, one launch (start us, length us, event | category | flops | bytes accessed | tf_op | source)
XLA Modules:
  0.0 535.2 jit_solution(4094026461271154416)
XLA Ops:
  6.5 0.0 copy-start.1
  6.5 0.9 dynamic-slice_convert_fusion.1
  7.4 0.2 mul.43
  7.7 0.5 copy-done.1
  8.1 0.7 fusion.2
  8.8 38.2 %psum.14 = f32[1024]{0:T(1024)S(1)} all-reduce(f32[1024]{0:T(1024)S(1)} %fusion.2), channel_id=1, replica_groups=mesh['row'=16,'col'=8] {'row'}, use_global_device_ids=true, to_apply=%region_2.0 | all-reduce | flops 1024 | bytes 8192 | tf_op jit(solution)/shard_map/psum | solution.py:77
  47.0 2.2 divide_convert_fusion
  49.3 0.0 copy-start
  49.3 6.2 %stack.2 = bf16[16,512,1024]{2,1,0:T(8,128)(2,1)} broadcast(bf16[512,1024]{1,0:T(8,128)(2,1)S(1)} %divide_convert_fusion), dimensions={1,2} | broadcast | bytes 17825792 | tf_op jit(solution)/shard_map/stack | solution.py:88
  55.4 0.0 copy-done
  55.5 0.0 copy-start.2
  55.5 5.3 all-to-all-start
  60.8 0.0 all-gather.2.cloned.1.call-start
  60.8 0.7 all-gather.2.cloned.1.call-update
  61.5 0.0 copy-done.2
  61.5 0.1 and_select_fusion.2
  61.6 0.8 dynamic-slice_convert_fusion
  62.4 0.1 select_reduce_fusion.2
  62.5 328.9 %all-gather.2.cloned.1.call-done = bf16[512,8192]{1,0:T(8,128)(2,1)} async-done(((bf16[512,1024]{1,0:T(8,128)(2,1)}), bf16[512,8192]{1,0:T(8,128)(2,1)}) %all-gather.2.cloned.1.call-update) | async-done | bytes 8388624 | tf_op jit(solution)/shard_map/all_gather | solution.py:79
  391.4 15.8 %all-to-all-done = bf16[16,512,1024]{2,1,0:T(8,128)(2,1)} async-done(((bf16[16,512,1024]{2,1,0:T(8,128)(2,1)}), bf16[16,512,1024]{2,1,0:T(8,128)(2,1)}, u32[]{:S(2)}, u32[]{:S(2)}) %all-to-all-start) | async-done | bytes 16777248 | tf_op jit(solution)/shard_map/all_to_all | solution.py:88
  407.2 0.2 mul.47
  407.4 14.8 %fusion.14 = (f32[1024]{0:T(1024)S(1)}, f32[512,1024]{1,0:T(8,128)S(1)}) fusion(f32[64,8,8,128]{3,2,1,0:T(8,128)S(1)} %bitcast.35, bf16[512,8192]{1,0:T(8,128)(2,1)} %all-gather.2.cloned.1.call-done, bf16[8192,1024]{1,0:T(8,128)(2,1)} %bitcast.1), kind=kOutput, calls=%fused_computation.43 | convolution fusion | flops 8591506432 | bytes 29364224 | tf_op jit(solution)/shard_map/dot_general | solution.py:85
  422.2 40.7 %psum.15 = f32[1024]{0:T(1024)S(1)} all-reduce(f32[1024]{0:T(1024)S(1)} %get-tuple-element.5), channel_id=1, replica_groups=mesh['row'=16,'col'=8] {'row'}, use_global_device_ids=true, to_apply=%region_4.5 | all-reduce | flops 1024 | bytes 8192 | tf_op jit(solution)/shard_map/psum | solution.py:93
  462.9 0.3 divide_bitcast_fusion
  463.2 0.5 copy.21
  463.7 1.9 fusion.5
  465.6 3.3 copy.12
  468.8 6.3 %all-to-all-start.1 = ((f32[16,512,128]{2,1,0:T(8,128)}), f32[16,512,128]{2,1,0:T(8,128)}, u32[]{:S(2)}, u32[]{:S(2)}) async-start(f32[16,512,128]{2,1,0:T(8,128)} %copy.12), calls=%async_computation.1 | async-start | bytes 8388608 | tf_op jit(solution)/shard_map/all_to_all | solution.py:95
  475.2 0.1 eq.99
  475.3 0.1 select_reduce_fusion.1
  475.4 0.1 broadcast_compare_fusion
  475.4 0.4 select_reduce_fusion
  475.8 0.1 copy.14
  475.9 43.8 %all-to-all-done.1 = f32[16,512,128]{2,1,0:T(8,128)} async-done(((f32[16,512,128]{2,1,0:T(8,128)}), f32[16,512,128]{2,1,0:T(8,128)}, u32[]{:S(2)}, u32[]{:S(2)}) %all-to-all-start.1) | async-done | bytes 4194336 | tf_op jit(solution)/shard_map/all_to_all | solution.py:95
  519.7 6.8 %fusion = f32[512,128,8]{1,2,0:T(8,128)S(1)} fusion(f32[8,16,1]{0,1,2:T(8,128)S(1)} %bitcast.36, f32[16,512,128]{2,1,0:T(8,128)} %all-to-all-done.1), kind=kOutput, calls=%fused_computation | convolution fusion | flops 100663296 | bytes 6291968 | tf_op jit(solution)/shard_map/sp,prb->rsb/dot_general | solution.py:54
  526.6 1.8 copy.33
  (6 shorter events, 0.0 us)
Async XLA Ops:
  6.5 1.6 copy-start.1
  49.3 6.2 %copy-start = (bf16[512,1024]{1,0:T(8,128)(2,1)}, bf16[512,1024]{1,0:T(8,128)(2,1)S(1)}, u32[]{:S(2)}) copy-start(bf16[512,1024]{1,0:T(8,128)(2,1)S(1)} %divide_convert_fusion) | copy-start | bytes 3145732
  55.5 6.0 %copy-start.2 = (s32[64]{0:T(128)S(1)}, s32[64]{0:T(128)}, u32[]{:S(2)}) copy-start(s32[64]{0:T(128)} %param.7) | copy-start | bytes 772
  55.5 351.8 %all-to-all-start = ((bf16[16,512,1024]{2,1,0:T(8,128)(2,1)}), bf16[16,512,1024]{2,1,0:T(8,128)(2,1)}, u32[]{:S(2)}, u32[]{:S(2)}) async-start(bf16[16,512,1024]{2,1,0:T(8,128)(2,1)} %stack.2), calls=%async_computation | async-start | bytes 33554432 | tf_op jit(solution)/shard_map/all_to_all | solution.py:88
  60.8 330.6 %all-gather.2.cloned.1.call-start = ((), (), s32[]{:S(2)}) async-start(), calls=%async_computation.2 | async-start | bytes 9437184 | tf_op jit(solution)/shard_map/all_gather | solution.py:79
  468.8 50.9 %all-to-all-start.1 = ((f32[16,512,128]{2,1,0:T(8,128)}), f32[16,512,128]{2,1,0:T(8,128)}, u32[]{:S(2)}, u32[]{:S(2)}) async-start(f32[16,512,128]{2,1,0:T(8,128)} %copy.12), calls=%async_computation.1 | async-start | bytes 8388608 | tf_op jit(solution)/shard_map/all_to_all | solution.py:95
Sparse Core Ops, SparseCore 0:
  63.2 328.1 all-gather.1
